TPU v7x, 32 devices: a whole 2x2x4 slice. The times are simulated.
32 devices in a mesh: groups: 2 (over x), out: 16 (over z, y, core).
Axes of the slice: x: 2, y: 2, z: 4, core: 2. Of those that a mesh axis runs over, the one named last changes fastest.
Arguments:
- tokens: bfloat16 [256, 8192], P('groups', 'out'), parts along dimension 0, may hold values from -60 to 60, as said below
- grad_hidden: bfloat16 [256, 16384], P('groups', 'out'), parts along dimension 0, may hold values from -6 to 6
- w_gate: bfloat16 [8192, 16384], P(None, 'out'), may hold values from -0.0625 to 0.0625
- w_up: bfloat16 [8192, 16384], P(None, 'out'), may hold values from -0.0625 to 0.0625
- a_factors: bfloat16 [8192, 128], replicated, may hold values from -0.0625 to 0.0625
- b_factors: bfloat16 [2, 64, 16384], P(None, None, 'out'), may hold values from -0.75 to 0.75
- magnitudes: float32 [2, 16384], P(None, 'out'), may hold values from 1 to 2
Outputs:
- hidden: bfloat16 [256, 16384], P('groups', 'out'), parts along dimension 0
- grad_tokens: bfloat16 [256, 8192], P('groups', 'out'), parts along dimension 0
- step_a: float32 [16384, 128], P(('groups', 'out')), parts along dimension 0
- step_b: float32 [4, 64, 16384], P('groups', None, 'out'), parts along dimension 0
- step_m: float32 [4, 16384], P('groups', 'out'), parts along dimension 0
There are 2 independent parts, one for each index of `groups`. A program takes and returns all parts, laid end to end along the dimension named above; an argument that names none is the same for every part. Nothing has to cross between parts.
Inputs may be any that keep to these rules, and one draw needn't show every extreme that they name: `tokens`: activations with feature scales that differ between features.
All inputs are finite; a program needn't handle non-finite values.
Results may differ from a plain program's by a relative error of at most 0.0073.
Values may be sent and summed in bfloat16 or wider, within the bound.
A program may use at most 128 MiB of HBM per device.

v0:
```python
import jax
import jax.numpy as jnp
from jax import lax
from jax.sharding import PartitionSpec as P

D = 8192
FW = 16384
R = 64


def inner_product(left_side, right_side, precision=None):
    return lax.dot_general(
        left_side,
        right_side,
        (((0,), (0,)), ((), ())),
        precision=precision,
        preferred_element_type=jnp.float32,
    )


def outer_contract(left_side, right_side, precision=None):
    return lax.dot_general(
        left_side,
        right_side,
        (((1,), (1,)), ((), ())),
        precision=precision,
        preferred_element_type=jnp.float32,
    )


def split_parts(values):
    upper = values.astype(jnp.bfloat16)
    lower = (values - upper.astype(jnp.float32)).astype(jnp.bfloat16)
    return (upper, lower)


def per_device(tokens, grad_hidden, w_gate, w_up, a_factors, b_factors, magnitudes):
    weights = (w_gate, w_up)
    rank = a_factors.shape[1] // 2
    count_tokens = tokens.shape[0]
    norms = []
    scales = []
    for which in range(2):
        weight = weights[which]
        left = a_factors[:, which * rank : (which + 1) * rank]
        right = b_factors[which]
        merged = weight.astype(jnp.float32) + jnp.dot(
            left, right, preferred_element_type=jnp.float32
        )
        squares = jnp.sum(merged * merged, axis=0)
        norm_col = jnp.sqrt(squares + 1e-06)
        norms.append(norm_col)
        scales.append(magnitudes[which] / norm_col)
    whole = lax.all_gather(tokens, "out", axis=1, tiled=True)
    base_gate = jnp.dot(whole, w_gate, preferred_element_type=jnp.float32)
    base_up = jnp.dot(whole, w_up, preferred_element_type=jnp.float32)
    low_wide = jnp.dot(whole, a_factors, preferred_element_type=jnp.float32)
    low = low_wide.astype(jnp.bfloat16)
    bases = []
    pres = []
    for which, raw in enumerate((base_gate, base_up)):
        base = raw + jnp.dot(
            low[:, which * rank : (which + 1) * rank],
            b_factors[which],
            preferred_element_type=jnp.float32,
        )
        bases.append(base)
        pres.append(base * scales[which][None, :])
    sigma = jax.nn.sigmoid(pres[0])
    hidden = (pres[0] * sigma * pres[1]).astype(jnp.bfloat16)
    cotangent = grad_hidden.astype(jnp.float32)
    dpres = (
        cotangent * pres[1] * sigma * (1.0 + pres[0] * (1.0 - sigma)),
        cotangent * pres[0] * sigma,
    )
    partial_sum = jnp.zeros((count_tokens, w_gate.shape[0]), jnp.float32)
    z_blocks = []
    grad_bs = []
    grad_ms = []
    for which in range(2):
        dscaled = (dpres[which] * scales[which][None, :]).astype(jnp.bfloat16)
        grad_ms.append(jnp.sum(dpres[which] * bases[which], axis=0) / norms[which])
        grad_bs.append(inner_product(low[:, which * rank : (which + 1) * rank], dscaled))
        z_blocks.append(outer_contract(dscaled, b_factors[which]))
        partial_sum = partial_sum + outer_contract(dscaled, weights[which])
    z_local = jnp.concatenate(z_blocks, axis=1)
    z_upper, z_lower = split_parts(z_local)
    partial_sum = (
        partial_sum + outer_contract(z_upper, a_factors) + outer_contract(z_lower, a_factors)
    )
    a_terms = inner_product(whole, z_upper) + inner_product(whole, z_lower)
    grad_a = lax.psum_scatter(a_terms, "out", scatter_dimension=0, tiled=True)
    summed_inputs = lax.psum_scatter(partial_sum, "out", scatter_dimension=1, tiled=True)
    grad_tokens = summed_inputs.astype(jnp.bfloat16)
    grad_b = jnp.stack(grad_bs)
    grad_m = jnp.stack(grad_ms)
    local_energy = jnp.sum(grad_a * grad_a) + jnp.sum(grad_b * grad_b) + jnp.sum(grad_m * grad_m)
    energy = lax.psum(local_energy, "out")
    count_all = 2 * D * R + 2 * R * FW + 2 * FW
    rms_value = jnp.sqrt(energy / count_all + 1e-06)
    return (hidden, grad_tokens, grad_a / rms_value, grad_b / rms_value, grad_m / rms_value)


def solution(mesh):
    in_specs = (
        P("groups", "out"),
        P("groups", "out"),
        P(None, "out"),
        P(None, "out"),
        P(),
        P(None, None, "out"),
        P(None, "out"),
    )
    out_specs = (
        P("groups", "out"),
        P("groups", "out"),
        P(("groups", "out"), None),
        P("groups", None, "out"),
        P("groups", "out"),
    )
    return jax.shard_map(
        per_device, mesh=mesh, in_specs=in_specs, out_specs=out_specs, check_vma=False
    )
```

profile of v0, /device:TPU:0, one launch (start us, length us, event | category | flops | bytes accessed | tf_op | source)
XLA Modules:
  0.0 230.4 jit_solution(6841040627441248489)
XLA Ops:
  7.2 0.0 all-gather.2.cloned.1.call-start
  7.2 0.7 all-gather.2.cloned.1.call-update
  7.9 0.0 copy-start.2
  7.9 0.0 copy-start.3
  7.9 0.0 reduce-scatter.5.cloned.1.call-start
  8.0 0.0 copy-start
  8.0 8.9 %multiply_reduce_fusion.1 = f32[1024]{0:T(1024)S(1)} fusion(bf16[8192,1024]{1,0:T(8,128)(2,1)} %param.9, bf16[8192,128]{1,0:T(8,128)(2,1)} %param.11, bf16[2,64,1024]{2,1,0:T(8,128)(2,1)} %param.12), kind=kOutput, calls=%fused_computation.1 | convolution fusion | flops 1107295232 | bytes 19009536 | tf_op jit(solution)/shard_map/dot_general | solution.py:47
  16.9 0.0 copy-done.2
  16.9 0.0 copy-done.3
  16.9 2.9 %copy-done = bf16[8192,1024]{1,0:T(8,128)(2,1)S(1)} copy-done((bf16[8192,1024]{1,0:T(8,128)(2,1)S(1)}, bf16[8192,1024]{1,0:T(8,128)(2,1)}, u32[]{:S(2)}) %copy-start) | copy-done | bytes 16777240
  19.8 5.5 %multiply_reduce_fusion = f32[1024]{0:T(1024)S(1)} fusion(bf16[8192,1024]{1,0:T(8,128)(2,1)S(1)} %copy-done, bf16[8192,128]{1,0:T(8,128)(2,1)S(1)} %copy-done.2, bf16[2,64,1024]{2,1,0:T(8,128)(2,1)S(1)} %copy-done.3), kind=kOutput, calls=%fused_computation | convolution fusion | flops 1107295232 | bytes 19009536 | tf_op jit(solution)/shard_map/dot_general | solution.py:47
  25.4 0.0 copy-done.4
  25.4 28.7 %all-gather.2.cloned.1.call-done = bf16[128,8192]{1,0:T(8,128)(2,1)} async-done(((bf16[128,512]{1,0:T(8,128)(2,1)}), bf16[128,8192]{1,0:T(8,128)(2,1)}) %all-gather.2.cloned.1.call-update) | async-done | bytes 2097168 | tf_op jit(solution)/shard_map/all_gather | solution.py:54
  54.1 2.7 %convolution_convert_fusion = bf16[128,128]{0,1:T(8,128)(2,1)S(1)} fusion(bf16[128,8192]{1,0:T(8,128)(2,1)} %all-gather.2.cloned.1.call-done, bf16[8192,128]{1,0:T(8,128)(2,1)S(1)} %copy-done.2), kind=kOutput, calls=%fused_computation.13 | convolution fusion | flops 268451840 | bytes 4227072 | tf_op jit(solution)/shard_map/dot_general | solution.py:57
  56.8 0.0 slice-start.1
  56.8 0.0 slice-start.2
  56.8 0.0 slice-start.3
  56.8 0.0 copy-start.1
  56.8 8.9 %fusion.32 = f32[128,1024]{1,0:T(8,128)S(1)} fusion(bf16[128,8192]{1,0:T(8,128)(2,1)} %all-gather.2.cloned.1.call-done, bf16[8192,1024]{1,0:T(8,128)(2,1)} %param.10), kind=kOutput, calls=%fused_computation.62 | convolution fusion | flops 2147483648 | bytes 19398656 | tf_op jit(solution)/shard_map/dot_general | solution.py:56
  65.7 0.2 convolution_add_fusion.4
  66.0 0.8 slice-done.3
  66.8 0.6 copy-done.1
  67.4 2.4 %fusion.31 = f32[128,1024]{1,0:T(8,128)S(1)} fusion(bf16[128,8192]{1,0:T(8,128)(2,1)S(1)} %copy-done.1, bf16[8192,1024]{1,0:T(8,128)(2,1)S(1)} %bitcast.47), kind=kOutput, calls=%fused_computation.61 | convolution fusion | flops 2147483648 | bytes 19398656 | tf_op jit(solution)/shard_map/dot_general | solution.py:55
  69.9 1.3 multiply_reduce_fusion.3
  71.2 0.2 fusion.11
  71.4 0.2 fusion.7
  71.6 0.7 fusion.26
  72.3 2.6 %fusion = f32[8192,128]{0,1:T(8,128)} fusion(f32[128,8192]{1,0:T(8,128)S(1)} %fusion.26, bf16[128,8192]{1,0:T(8,128)(2,1)S(1)} %copy-done.1, f32[128,64]{0,1:T(8,128)S(1)} %fusion.7, f32[128,64]{0,1:T(8,128)S(1)} %fusion.11), kind=kOutput, calls=%fused_computation.3 | convolution fusion | flops 269565952 | bytes 10551296 | tf_op jit(solution)/shard_map/dot_general | solution.py:12
  75.0 0.0 reduce-scatter.5.cloned.1.call-update
  75.0 0.3 reduce-scatter.3.cloned.1.call-start
  75.3 13.5 %fusion.33 = f32[128,8192]{1,0:T(8,128)} fusion(bf16[128,1024]{1,0:T(8,128)(2,1)S(1)} %get-tuple-element.12, bf16[8192,1024]{1,0:T(8,128)(2,1)} %param.9), kind=kOutput, calls=%fused_computation.63 | convolution fusion | flops 2147483648 | bytes 21233664 | tf_op jit(solution)/shard_map/dot_general | solution.py:22
  88.8 15.3 %convolution_add_fusion.3 = f32[128,8192]{1,0:T(8,128)} fusion(f32[128,8192]{1,0:T(8,128)} %fusion.33, bf16[128,1024]{1,0:T(8,128)(2,1)S(1)} %get-tuple-element.14, bf16[8192,1024]{1,0:T(8,128)(2,1)} %param.10), kind=kOutput, calls=%fused_computation.6 | convolution fusion | flops 2148532224 | bytes 25427968 | tf_op jit(solution)/shard_map/dot_general | solution.py:22
  104.1 3.0 %convolution_add_fusion.2 = f32[128,8192]{1,0:T(8,128)S(1)} fusion(f32[128,8192]{1,0:T(8,128)} %convolution_add_fusion.3, bf16[8192,128]{1,0:T(8,128)(2,1)S(1)} %copy-done.2, f32[128,64]{0,1:T(8,128)S(1)} %fusion.7, f32[128,64]{0,1:T(8,128)S(1)} %fusion.11), kind=kOutput, calls=%fused_computation.5 | convolution fusion | flops 269549568 | bytes 10551296 | tf_op jit(solution)/shard_map/dot_general | solution.py:22
  107.1 2.8 %convolution_add_fusion.1 = f32[128,8192]{1,0:T(8,128)} fusion(f32[128,8192]{1,0:T(8,128)S(1)} %convolution_add_fusion.2, bf16[8192,128]{1,0:T(8,128)(2,1)S(1)} %copy-done.2, f32[128,64]{0,1:T(8,128)S(1)} %fusion.7, f32[128,64]{0,1:T(8,128)S(1)} %fusion.11), kind=kOutput, calls=%fused_computation.4 | convolution fusion | flops 269565952 | bytes 10551296 | tf_op jit(solution)/shard_map/dot_general | solution.py:22
  109.8 0.0 reduce-scatter.3.cloned.1.call-update
  109.9 0.6 multiply_reduce_fusion.6
  110.5 0.2 convolution_bitcast_fusion
  110.7 0.2 convolution_bitcast_fusion.1
  110.9 0.7 multiply_reduce_fusion.4
  111.6 34.9 %reduce-scatter.5.cloned.1.call-done = f32[512,128]{0,1:T(8,128)} async-done(((f32[8192,128]{0,1:T(8,128)}), f32[512,128]{0,1:T(8,128)}) %reduce-scatter.5.cloned.1.call-update) | async-done | bytes 262160 | tf_op jit(solution)/shard_map/reduce_scatter | solution.py:92
  146.5 1.6 multiply_reduce_fusion.5
  150.1 30.5 %psum.7 = f32[]{:T(128)} all-reduce(f32[]{:T(128)S(6)} %add.92), channel_id=1, replica_groups=mesh['groups'=2,'out'=16] {'out'}, use_global_device_ids=true, to_apply=%region_9.0 | all-reduce | flops 1 | bytes 8 | tf_op jit(solution)/shard_map/psum | solution.py:98
  181.3 1.0 broadcast_divide_fusion
  182.3 0.8 copy.12
  183.1 0.6 broadcast_divide_fusion.1
  183.8 0.9 fusion.6
  184.6 37.7 %reduce-scatter.3.cloned.1.call-done = f32[128,512]{1,0:T(8,128)} async-done(((f32[128,8192]{1,0:T(8,128)}), f32[128,512]{1,0:T(8,128)}) %reduce-scatter.3.cloned.1.call-update) | async-done | bytes 262160 | tf_op jit(solution)/shard_map/reduce_scatter | solution.py:93
  222.3 1.6 convert_element_type.43
  (13 shorter events, 0.1 us)
Async XLA Ops:
  7.2 46.9 %all-gather.2.cloned.1.call-start = ((), (), s32[]{:S(2)}) async-start(), calls=%async_computation.2 | async-start | bytes 2228224 | tf_op jit(solution)/shard_map/all_gather | solution.py:54
  7.9 9.0 %copy-start.2 = (bf16[8192,128]{1,0:T(8,128)(2,1)S(1)}, bf16[8192,128]{1,0:T(8,128)(2,1)}, u32[]{:S(2)}) copy-start(bf16[8192,128]{1,0:T(8,128)(2,1)} %param.11) | copy-start | bytes 6291460
  7.9 9.0 %copy-start.3 = (bf16[2,64,1024]{2,1,0:T(8,128)(2,1)S(1)}, bf16[2,64,1024]{2,1,0:T(8,128)(2,1)}, u32[]{:S(2)}) copy-start(bf16[2,64,1024]{2,1,0:T(8,128)(2,1)} %param.12) | copy-start | bytes 786436
  7.9 138.6 %reduce-scatter.5.cloned.1.call-start = ((), (), s32[]{:S(2)}) async-start(), calls=%async_computation.4 | async-start | bytes 4456448 | tf_op jit(solution)/shard_map/reduce_scatter | solution.py:92
  8.0 11.9 %copy-start = (bf16[8192,1024]{1,0:T(8,128)(2,1)S(1)}, bf16[8192,1024]{1,0:T(8,128)(2,1)}, u32[]{:S(2)}) copy-start(bf16[8192,1024]{1,0:T(8,128)(2,1)} %param.10) | copy-start | bytes 50331652
  19.8 5.6 %copy-start.4 = (f32[2,1024]{1,0:T(2,128)S(1)}, f32[2,1024]{1,0:T(2,128)}, u32[]{:S(2)}) copy-start(f32[2,1024]{1,0:T(2,128)} %param.13) | copy-start | bytes 24580
  54.1 11.9 %slice-start = ((s8[16777216]{0:T(1024)(128)(4,1)}), s8[4194304]{0:T(1024)(128)(4,1)S(1)}, s32[]{:S(2)}) async-start(s8[16777216]{0:T(1024)(128)(4,1)} %bitcast.46), calls=%async_computation.5 | async-start | bytes 8388608
  56.8 9.2 %slice-start.1 = ((s8[16777216]{0:T(1024)(128)(4,1)}), s8[4194304]{0:T(1024)(128)(4,1)S(1)}, s32[]{:S(2)}) async-start(s8[16777216]{0:T(1024)(128)(4,1)} %bitcast.46), calls=%async_computation.6 | async-start | bytes 8388608
  56.8 9.2 %slice-start.2 = ((s8[16777216]{0:T(1024)(128)(4,1)}), s8[4194304]{0:T(1024)(128)(4,1)S(1)}, s32[]{:S(2)}) async-start(s8[16777216]{0:T(1024)(128)(4,1)} %bitcast.46), calls=%async_computation.7 | async-start | bytes 8388608
  56.8 10.0 %slice-start.3 = ((s8[16777216]{0:T(1024)(128)(4,1)}), s8[4194304]{0:T(1024)(128)(4,1)S(1)}, s32[]{:S(2)}) async-start(s8[16777216]{0:T(1024)(128)(4,1)} %bitcast.46), calls=%async_computation.8 | async-start | bytes 8388608
  56.8 10.6 %copy-start.1 = (bf16[128,8192]{1,0:T(8,128)(2,1)S(1)}, bf16[128,8192]{1,0:T(8,128)(2,1)}, u32[]{:S(2)}) copy-start(bf16[128,8192]{1,0:T(8,128)(2,1)} %all-gather.2.cloned.1.call-done) | copy-start | bytes 6291460
  67.4 2.5 %copy-start.5 = (bf16[128,1024]{1,0:T(8,128)(2,1)S(1)}, bf16[128,1024]{1,0:T(8,128)(2,1)}, u32[]{:S(2)}) copy-start(bf16[128,1024]{1,0:T(8,128)(2,1)} %param.8) | copy-start | bytes 786436
  75.0 147.3 %reduce-scatter.3.cloned.1.call-start = ((), (), s32[]{:S(2)}) async-start(), calls=%async_computation.3 | async-start | bytes 4456448 | tf_op jit(solution)/shard_map/reduce_scatter | solution.py:93
Sparse Core Ops, SparseCore 0:
  10.2 43.8 all-gather.1
  75.1 71.3 reduce-scatter.4
  150.9 71.3 reduce-scatter.2
where the time goes:
time: 231 us; the launch traced here: 230 us
  waiting for transfers between devices  102 us (44%)
  matrix products  68.7 us (30%)
  blocking collectives  30.5 us (13%)
  between operations  16.6 us (7%)
  other arithmetic  7.07 us (3%)
  local copies, waits for them, and re-layouts  5.15 us (2%)
    reduce_scatter x1, waiting for transfers between devices, per_device(): lax.psum_scatter(partial_sum, 'out', scatter_dimension=1, tiled=True)  37.7 us
    dot_general x6, matrix products, outer_contract(): lax.dot_general(left_side, right_side, (((1,), (1,)), ((), ())), precisio...  35 us
    reduce_scatter x1, waiting for transfers between devices, per_device(): grad_a = lax.psum_scatter(a_terms, 'out', scatter_dimension=0, tiled=True)  34.9 us
    psum x1, blocking collectives, per_device(): energy = lax.psum(local_energy, 'out')  30.5 us
    all_gather x1, waiting for transfers between devices, per_device(): whole = lax.all_gather(tokens, 'out', axis=1, tiled=True)  28.7 us
    dot_general x2, matrix products, per_device(): jnp.dot(left, right, preferred_element_type=jnp.float32)  14.5 us
    dot_general x1, matrix products, per_device(): base_up = jnp.dot(whole, w_up, preferred_element_type=jnp.float32)  8.88 us
    unnamed x21, local copies, waits for them, and re-layouts  5.15 us
  transfers between devices with their start and end apart: 3, of which 3 were waited for; matrix products, arithmetic and copies ran while one was open for 24% of the time, Pallas kernels for 0%

commit v1 on v0

--- a/solution.py
+++ b/solution.py
@@ -6,6 +6,29 @@
 D = 8192
 FW = 16384
 R = 64
+
+
+def assign_bars(original):
+    mixed_arr = lax.axis_size("out")
+    built = lax.axis_index("out")
+    s_next, earlier, block_next = (mixed_arr, built, original.shape[1])
+    block_list = tuple((q * s_next if src_i == 1 else q for src_i, q in enumerate(original.shape)))
+    shaped = jnp.zeros(block_list, original.dtype)
+    z2 = lax.dynamic_update_slice_in_dim(shaped, original, earlier * block_next, axis=1)
+    part_now = piece_next = original
+    for dev_i in range(1, s_next // 2 + 1):
+        all_values = tuple(((src_i, (src_i + 1) % s_next) for src_i in range(s_next)))
+        part_now = lax.ppermute(part_now, "out", all_values)
+        z2 = lax.dynamic_update_slice_in_dim(
+            z2, part_now, (earlier - dev_i) % s_next * block_next, axis=1
+        )
+        if 2 * dev_i < s_next:
+            z_new = tuple(((src_i, (src_i - 1) % s_next) for src_i in range(s_next)))
+            piece_next = lax.ppermute(piece_next, "out", z_new)
+            z2 = lax.dynamic_update_slice_in_dim(
+                z2, piece_next, (earlier + dev_i) % s_next * block_next, axis=1
+            )
+    return z2
 
 
 def inner_product(left_side, right_side, precision=None):
@@ -51,7 +74,7 @@
         norm_col = jnp.sqrt(squares + 1e-06)
         norms.append(norm_col)
         scales.append(magnitudes[which] / norm_col)
-    whole = lax.all_gather(tokens, "out", axis=1, tiled=True)
+    whole = assign_bars(tokens)
     base_gate = jnp.dot(whole, w_gate, preferred_element_type=jnp.float32)
     base_up = jnp.dot(whole, w_up, preferred_element_type=jnp.float32)
     low_wide = jnp.dot(whole, a_factors, preferred_element_type=jnp.float32)

time: 231 us -> 253 us (1.095)
  starting transfers between devices: 0.34 us -> 32.7 us
  waiting for transfers between devices: 102 us -> 95.7 us
  local copies, waits for them, and re-layouts: 5.15 us -> 1.84 us
    ppermute x0 -> x15, starting transfers between devices: none -> 32.4 us  [the longest x7 31.8 us: assign_bars(): piece_next = lax.ppermute(piece_next, 'out', z_new)]
    all_gather x1 -> x0, waiting for transfers between devices: 28.7 us -> none  [per_device(): whole = lax.all_gather(tokens, 'out', axis=1, tiled=True)]
    ppermute x0 -> x15, waiting for transfers between devices: none -> 23 us  [the longest x8 23 us: assign_bars(): part_now = lax.ppermute(part_now, 'out', all_values)]
    unnamed x21 -> x20, local copies, waits for them, and re-layouts: 5.15 us -> 1.42 us
  transfers between devices with their start and end apart: 3 -> 17, of which waited for: 3 -> 9; matrix products, arithmetic and copies ran while one was open for 24% -> 22% of each run, Pallas kernels for 0% -> 0%
where the time goes in v1:
time: 253 us; the launch traced here: 252 us
  waiting for transfers between devices  95.7 us (38%)
  matrix products  66.5 us (26%)
  starting transfers between devices  32.7 us (13%)
  blocking collectives  30.6 us (12%)
  between operations  17.4 us (7%)
  other arithmetic  7.77 us (3%)
    reduce_scatter x1, waiting for transfers between devices, per_device(): lax.psum_scatter(partial_sum, 'out', scatter_dimension=1, tiled=True)  38 us
    dot_general x6, matrix products, outer_contract(): lax.dot_general(left_side, right_side, (((1,), (1,)), ((), ())), precisio...  35 us
    reduce_scatter x1, waiting for transfers between devices, per_device(): grad_a = lax.psum_scatter(a_terms, 'out', scatter_dimension=0, tiled=True)  34.7 us
    ppermute x7, starting transfers between devices, assign_bars(): piece_next = lax.ppermute(piece_next, 'out', z_new)  31.8 us
    psum x1, blocking collectives, per_device(): energy = lax.psum(local_energy, 'out')  30.6 us
    ppermute x8, waiting for transfers between devices, assign_bars(): part_now = lax.ppermute(part_now, 'out', all_values)  23 us
    dot_general x2, matrix products, per_device(): jnp.dot(left, right, preferred_element_type=jnp.float32)  14.1 us
    dot_general x1, matrix products, per_device(): base_up = jnp.dot(whole, w_up, preferred_element_type=jnp.float32)  8.43 us
  transfers between devices with their start and end apart: 17, of which 9 were waited for; matrix products, arithmetic and copies ran while one was open for 22% of the time, Pallas kernels for 0%

profile of v1, /device:TPU:0, one launch (start us, length us, event | category | flops | bytes accessed | tf_op | source)
XLA Modules:
  0.0 252.4 jit_solution(1906558172333029101)
XLA Ops:
  7.2 0.0 reduce-scatter.5.cloned.1.call-start
  7.2 0.5 collective-permute-start
  7.7 5.1 %collective-permute-start.1 = (bf16[128,512]{1,0:T(8,128)(2,1)}, bf16[128,512]{1,0:T(8,128)(2,1)S(1)}, u32[]{:S(2)}, u32[]{:S(2)}) collective-permute-start(bf16[128,512]{1,0:T(8,128)(2,1)} %param.7), channel_id=1, source_target_pairs={{0,15},{1,0},{2,1},{3,2},{4,3},{5,4},{6,5},{7,6},{8,7},{9,8},{10,9... | collective-permute-start | bytes 393224 | tf_op jit(solution)/shard_map/ppermute | solution.py:27
  12.8 8.8 %multiply_reduce_fusion.1 = f32[1024]{0:T(1024)S(1)} fusion(bf16[8192,1024]{1,0:T(8,128)(2,1)} %param.9, bf16[8192,128]{1,0:T(8,128)(2,1)} %param.11, bf16[2,64,1024]{2,1,0:T(8,128)(2,1)} %param.12), kind=kOutput, calls=%fused_computation.1 | convolution fusion | flops 1107295232 | bytes 19009536 | tf_op jit(solution)/shard_map/dot_general | solution.py:70
  21.7 5.3 %multiply_reduce_fusion = f32[1024]{0:T(1024)S(1)} fusion(bf16[8192,1024]{1,0:T(8,128)(2,1)S(1)} %copy-done, bf16[8192,128]{1,0:T(8,128)(2,1)S(1)} %copy-done.1, bf16[2,64,1024]{2,1,0:T(8,128)(2,1)S(1)} %copy-done.2), kind=kOutput, calls=%fused_computation | convolution fusion | flops 1107295232 | bytes 19009536 | tf_op jit(solution)/shard_map/dot_general | solution.py:70
  27.4 0.2 broadcast_in_dim.2
  27.6 0.4 copy-done.3
  27.9 0.1 collective-permute-start.2
  28.0 4.4 %collective-permute-start.3 = (bf16[128,512]{1,0:T(8,128)(2,1)S(1)}, bf16[128,512]{1,0:T(8,128)(2,1)S(1)}, u32[]{:S(2)}, u32[]{:S(2)}) collective-permute-start(bf16[128,512]{1,0:T(8,128)(2,1)S(1)} %collective-permute-done.1), channel_id=1, source_target_pairs={{0,15},{1,0},{2,1},{3,2},{4,3},{5,4},{6,5},{7,6},{8,7},{9,8},{10,9... | collective-permute-start | bytes 393224 | tf_op jit(solution)/shard_map/ppermute | solution.py:27
  32.5 2.6 %collective-permute-done.2 = bf16[128,512]{1,0:T(8,128)(2,1)S(1)} collective-permute-done((bf16[128,512]{1,0:T(8,128)(2,1)S(1)}, bf16[128,512]{1,0:T(8,128)(2,1)S(1)}, u32[]{:S(2)}, u32[]{:S(2)}) %collective-permute-start.2) | collective-permute-done | bytes 131104 | tf_op jit(solution)/shard_map/ppermute | solution.py:21
  35.1 4.5 %collective-permute-start.5 = (bf16[128,512]{1,0:T(8,128)(2,1)S(1)}, bf16[128,512]{1,0:T(8,128)(2,1)S(1)}, u32[]{:S(2)}, u32[]{:S(2)}) collective-permute-start(bf16[128,512]{1,0:T(8,128)(2,1)S(1)} %collective-permute-done.3), channel_id=1, source_target_pairs={{0,15},{1,0},{2,1},{3,2},{4,3},{5,4},{6,5},{7,6},{8,7},{9,8},{10,9... | collective-permute-start | bytes 393224 | tf_op jit(solution)/shard_map/ppermute | solution.py:27
  39.7 2.6 %collective-permute-done.4 = bf16[128,512]{1,0:T(8,128)(2,1)S(1)} collective-permute-done((bf16[128,512]{1,0:T(8,128)(2,1)S(1)}, bf16[128,512]{1,0:T(8,128)(2,1)S(1)}, u32[]{:S(2)}, u32[]{:S(2)}) %collective-permute-start.4) | collective-permute-done | bytes 131104 | tf_op jit(solution)/shard_map/ppermute | solution.py:21
  42.3 4.4 %collective-permute-start.7 = (bf16[128,512]{1,0:T(8,128)(2,1)S(1)}, bf16[128,512]{1,0:T(8,128)(2,1)S(1)}, u32[]{:S(2)}, u32[]{:S(2)}) collective-permute-start(bf16[128,512]{1,0:T(8,128)(2,1)S(1)} %collective-permute-done.5), channel_id=1, source_target_pairs={{0,15},{1,0},{2,1},{3,2},{4,3},{5,4},{6,5},{7,6},{8,7},{9,8},{10,9... | collective-permute-start | bytes 393224 | tf_op jit(solution)/shard_map/ppermute | solution.py:27
  46.8 2.7 %collective-permute-done.6 = bf16[128,512]{1,0:T(8,128)(2,1)S(1)} collective-permute-done((bf16[128,512]{1,0:T(8,128)(2,1)S(1)}, bf16[128,512]{1,0:T(8,128)(2,1)S(1)}, u32[]{:S(2)}, u32[]{:S(2)}) %collective-permute-start.6) | collective-permute-done | bytes 131104 | tf_op jit(solution)/shard_map/ppermute | solution.py:21
  49.5 4.4 %collective-permute-start.9 = (bf16[128,512]{1,0:T(8,128)(2,1)S(1)}, bf16[128,512]{1,0:T(8,128)(2,1)S(1)}, u32[]{:S(2)}, u32[]{:S(2)}) collective-permute-start(bf16[128,512]{1,0:T(8,128)(2,1)S(1)} %collective-permute-done.7), channel_id=1, source_target_pairs={{0,15},{1,0},{2,1},{3,2},{4,3},{5,4},{6,5},{7,6},{8,7},{9,8},{10,9... | collective-permute-start | bytes 393224 | tf_op jit(solution)/shard_map/ppermute | solution.py:27
  54.0 2.7 %collective-permute-done.8 = bf16[128,512]{1,0:T(8,128)(2,1)S(1)} collective-permute-done((bf16[128,512]{1,0:T(8,128)(2,1)S(1)}, bf16[128,512]{1,0:T(8,128)(2,1)S(1)}, u32[]{:S(2)}, u32[]{:S(2)}) %collective-permute-start.8) | collective-permute-done | bytes 131104 | tf_op jit(solution)/shard_map/ppermute | solution.py:21
  56.7 4.4 %collective-permute-start.11 = (bf16[128,512]{1,0:T(8,128)(2,1)S(1)}, bf16[128,512]{1,0:T(8,128)(2,1)S(1)}, u32[]{:S(2)}, u32[]{:S(2)}) collective-permute-start(bf16[128,512]{1,0:T(8,128)(2,1)S(1)} %collective-permute-done.9), channel_id=1, source_target_pairs={{0,15},{1,0},{2,1},{3,2},{4,3},{5,4},{6,5},{7,6},{8,7},{9,8},{10,9... | collective-permute-start | bytes 393224 | tf_op jit(solution)/shard_map/ppermute | solution.py:27
  61.2 2.7 %collective-permute-done.10 = bf16[128,512]{1,0:T(8,128)(2,1)S(1)} collective-permute-done((bf16[128,512]{1,0:T(8,128)(2,1)S(1)}, bf16[128,512]{1,0:T(8,128)(2,1)S(1)}, u32[]{:S(2)}, u32[]{:S(2)}) %collective-permute-start.10) | collective-permute-done | bytes 131104 | tf_op jit(solution)/shard_map/ppermute | solution.py:21
  63.9 4.4 %collective-permute-start.13 = (bf16[128,512]{1,0:T(8,128)(2,1)S(1)}, bf16[128,512]{1,0:T(8,128)(2,1)S(1)}, u32[]{:S(2)}, u32[]{:S(2)}) collective-permute-start(bf16[128,512]{1,0:T(8,128)(2,1)S(1)} %collective-permute-done.11), channel_id=1, source_target_pairs={{0,15},{1,0},{2,1},{3,2},{4,3},{5,4},{6,5},{7,6},{8,7},{9,8},{10,9... | collective-permute-start | bytes 393224 | tf_op jit(solution)/shard_map/ppermute | solution.py:27
  68.4 2.6 %collective-permute-done.12 = bf16[128,512]{1,0:T(8,128)(2,1)S(1)} collective-permute-done((bf16[128,512]{1,0:T(8,128)(2,1)S(1)}, bf16[128,512]{1,0:T(8,128)(2,1)S(1)}, u32[]{:S(2)}, u32[]{:S(2)}) %collective-permute-start.12) | collective-permute-done | bytes 131104 | tf_op jit(solution)/shard_map/ppermute | solution.py:21
  71.0 7.0 %collective-permute-done.14 = bf16[128,512]{1,0:T(8,128)(2,1)S(1)} collective-permute-done((bf16[128,512]{1,0:T(8,128)(2,1)S(1)}, bf16[128,512]{1,0:T(8,128)(2,1)S(1)}, u32[]{:S(2)}, u32[]{:S(2)}) %collective-permute-start.14) | collective-permute-done | bytes 131104 | tf_op jit(solution)/shard_map/ppermute | solution.py:21
  78.1 1.0 convolution_convert_fusion
  79.1 0.2 fusion.9
  79.3 0.2 fusion.14
  79.6 8.4 %convolution_add_fusion.4 = f32[128,1024]{1,0:T(8,128)S(1)} fusion(f32[128,1024]{1,0:T(8,128)S(1)} %fusion.9, bf16[128,8192]{1,0:T(8,128)(2,1)S(1)} %constant_dynamic-update-slice_fusion, bf16[8192,1024]{1,0:T(8,128)(2,1)} %param.10), kind=kOutput, calls=%fused_computation.8 | convolution fusion | flops 2147614720 | bytes 19922944 | tf_op jit(solution)/shard_map/dot_general | solution.py:79
  88.1 1.0 slice-done.3
  89.1 3.6 %multiply_reduce_fusion.3 = (f32[1024]{0:T(1024)S(1)}, f32[1024]{0:T(1024)S(1)}, bf16[128,1024]{1,0:T(8,128)(2,1)S(1)}, bf16[128,1024]{1,0:T(8,128)(2,1)}, bf16[128,1024]{1,0:T(8,128)(2,1)S(1)}) fusion(f32[1024]{0:T(1024)S(1)} %bitcast.50, f32[128,1024]{1,0:T(8,128)S(1)} %convolution_add_fusion.4, f32[1024]{0:T(1024)S(1)} %bitcast.51, ...), kind=kOutput, calls=%fused_computation.20 | convolution fusion | flops 2150889472 | bytes 20987904 | tf_op jit(solution)/shard_map/dot_general | solution.py:78
  92.7 0.2 fusion.6
  92.9 0.2 fusion.11
  93.1 0.7 fusion.31
  93.9 2.8 %convolution_add_fusion = f32[8192,128]{1,0:T(8,128)} fusion(f32[8192,128]{1,0:T(8,128)S(1)} %fusion.31, bf16[128,8192]{1,0:T(8,128)(2,1)S(1)} %constant_dynamic-update-slice_fusion, f32[128,64]{0,1:T(8,128)S(1)} %fusion.6, f32[128,64]{0,1:T(8,128)S(1)} %fusion.11), kind=kOutput, calls=%fused_computation.2 | convolution fusion | flops 269549568 | bytes 10551296 | tf_op jit(solution)/shard_map/dot_general | solution.py:35
  96.7 0.3 reduce-scatter.3.cloned.1.call-start
  97.0 13.6 %fusion.32 = f32[128,8192]{1,0:T(8,128)} fusion(bf16[128,1024]{1,0:T(8,128)(2,1)S(1)} %get-tuple-element.7, bf16[8192,1024]{1,0:T(8,128)(2,1)} %param.9), kind=kOutput, calls=%fused_computation.78 | convolution fusion | flops 2147483648 | bytes 21233664 | tf_op jit(solution)/shard_map/dot_general | solution.py:45
  110.6 15.2 %convolution_add_fusion.3 = f32[128,8192]{1,0:T(8,128)} fusion(f32[128,8192]{1,0:T(8,128)} %fusion.32, bf16[128,1024]{1,0:T(8,128)(2,1)S(1)} %get-tuple-element.9, bf16[8192,1024]{1,0:T(8,128)(2,1)} %param.10), kind=kOutput, calls=%fused_computation.5 | convolution fusion | flops 2148532224 | bytes 25427968 | tf_op jit(solution)/shard_map/dot_general | solution.py:45
  125.8 2.9 %convolution_add_fusion.2 = f32[128,8192]{1,0:T(8,128)S(1)} fusion(f32[128,8192]{1,0:T(8,128)} %convolution_add_fusion.3, bf16[8192,128]{1,0:T(8,128)(2,1)S(1)} %copy-done.1, f32[128,64]{0,1:T(8,128)S(1)} %fusion.6, f32[128,64]{0,1:T(8,128)S(1)} %fusion.11), kind=kOutput, calls=%fused_computation.4 | convolution fusion | flops 269549568 | bytes 10551296 | tf_op jit(solution)/shard_map/dot_general | solution.py:45
  128.7 2.8 %convolution_add_fusion.1 = f32[128,8192]{1,0:T(8,128)} fusion(f32[128,8192]{1,0:T(8,128)S(1)} %convolution_add_fusion.2, bf16[8192,128]{1,0:T(8,128)(2,1)S(1)} %copy-done.1, f32[128,64]{0,1:T(8,128)S(1)} %fusion.6, f32[128,64]{0,1:T(8,128)S(1)} %fusion.11), kind=kOutput, calls=%fused_computation.3 | convolution fusion | flops 269565952 | bytes 10551296 | tf_op jit(solution)/shard_map/dot_general | solution.py:45
  131.6 0.6 multiply_reduce_fusion.6
  132.2 0.2 convolution_bitcast_fusion
  132.4 0.2 convolution_bitcast_fusion.1
  132.6 0.7 multiply_reduce_fusion.4
  133.3 34.7 %reduce-scatter.5.cloned.1.call-done = f32[512,128]{1,0:T(8,128)} async-done(((f32[8192,128]{1,0:T(8,128)}), f32[512,128]{1,0:T(8,128)}) %reduce-scatter.5.cloned.1.call-update) | async-done | bytes 262160 | tf_op jit(solution)/shard_map/reduce_scatter | solution.py:115
  168.0 1.6 multiply_reduce_fusion.5
  171.5 30.6 %psum.7 = f32[]{:T(128)} all-reduce(f32[]{:T(128)S(6)} %add.249), channel_id=1, replica_groups=mesh['groups'=2,'out'=16] {'out'}, use_global_device_ids=true, to_apply=%region_9.10 | all-reduce | flops 1 | bytes 8 | tf_op jit(solution)/shard_map/psum | solution.py:121
  202.8 0.6 broadcast_divide_fusion.1
  203.4 0.8 fusion.5
  204.3 1.7 broadcast_divide_fusion
  205.9 38.0 %reduce-scatter.3.cloned.1.call-done = f32[128,512]{1,0:T(8,128)} async-done(((f32[128,8192]{1,0:T(8,128)}), f32[128,512]{1,0:T(8,128)}) %reduce-scatter.3.cloned.1.call-update) | async-done | bytes 262160 | tf_op jit(solution)/shard_map/reduce_scatter | solution.py:116
  244.0 1.6 convert_element_type.43
  (56 shorter events, 0.4 us)
Async XLA Ops:
  7.2 14.4 %copy-start.1 = (bf16[8192,128]{1,0:T(8,128)(2,1)S(1)}, bf16[8192,128]{1,0:T(8,128)(2,1)}, u32[]{:S(2)}) copy-start(bf16[8192,128]{1,0:T(8,128)(2,1)} %param.11) | copy-start | bytes 6291460
  7.2 14.4 %copy-start.2 = (bf16[2,64,1024]{2,1,0:T(8,128)(2,1)S(1)}, bf16[2,64,1024]{2,1,0:T(8,128)(2,1)}, u32[]{:S(2)}) copy-start(bf16[2,64,1024]{2,1,0:T(8,128)(2,1)} %param.12) | copy-start | bytes 786436
  7.2 160.8 %reduce-scatter.5.cloned.1.call-start = ((), (), s32[]{:S(2)}) async-start(), calls=%async_computation.3 | async-start | bytes 4456448 | tf_op jit(solution)/shard_map/reduce_scatter | solution.py:115
  7.2 14.4 %copy-start = (bf16[8192,1024]{1,0:T(8,128)(2,1)S(1)}, bf16[8192,1024]{1,0:T(8,128)(2,1)}, u32[]{:S(2)}) copy-start(bf16[8192,1024]{1,0:T(8,128)(2,1)} %param.10) | copy-start | bytes 50331652
  7.2 20.7 %collective-permute-start = (bf16[128,512]{1,0:T(8,128)(2,1)}, bf16[128,512]{1,0:T(8,128)(2,1)S(1)}, u32[]{:S(2)}, u32[]{:S(2)}) collective-permute-start(bf16[128,512]{1,0:T(8,128)(2,1)} %param.7), channel_id=1, source_target_pairs={{0,1},{1,2},{2,3},{3,4},{4,5},{5,6},{6,7},{7,8},{8,9},{9,10},{10,1... | collective-permute-start | bytes 393224 | tf_op jit(solution)/shard_map/ppermute | solution.py:21
  7.7 20.3 %collective-permute-start.1 = (bf16[128,512]{1,0:T(8,128)(2,1)}, bf16[128,512]{1,0:T(8,128)(2,1)S(1)}, u32[]{:S(2)}, u32[]{:S(2)}) collective-permute-start(bf16[128,512]{1,0:T(8,128)(2,1)} %param.7), channel_id=1, source_target_pairs={{0,15},{1,0},{2,1},{3,2},{4,3},{5,4},{6,5},{7,6},{8,7},{9,8},{10,9... | collective-permute-start | bytes 393224 | tf_op jit(solution)/shard_map/ppermute | solution.py:27
  21.6 5.4 %copy-start.4 = (f32[2,1024]{1,0:T(2,128)S(1)}, f32[2,1024]{1,0:T(2,128)}, u32[]{:S(2)}) copy-start(f32[2,1024]{1,0:T(2,128)} %param.13) | copy-start | bytes 24580
  27.0 0.9 copy-start.3
  27.9 7.1 %collective-permute-start.2 = (bf16[128,512]{1,0:T(8,128)(2,1)S(1)}, bf16[128,512]{1,0:T(8,128)(2,1)S(1)}, u32[]{:S(2)}, u32[]{:S(2)}) collective-permute-start(bf16[128,512]{1,0:T(8,128)(2,1)S(1)} %collective-permute-done), channel_id=1, source_target_pairs={{0,1},{1,2},{2,3},{3,4},{4,5},{5,6},{6,7},{7,8},{8,9},{9,10},{10,1... | collective-permute-start | bytes 393224 | tf_op jit(solution)/shard_map/ppermute | solution.py:21
  28.0 7.1 %collective-permute-start.3 = (bf16[128,512]{1,0:T(8,128)(2,1)S(1)}, bf16[128,512]{1,0:T(8,128)(2,1)S(1)}, u32[]{:S(2)}, u32[]{:S(2)}) collective-permute-start(bf16[128,512]{1,0:T(8,128)(2,1)S(1)} %collective-permute-done.1), channel_id=1, source_target_pairs={{0,15},{1,0},{2,1},{3,2},{4,3},{5,4},{6,5},{7,6},{8,7},{9,8},{10,9... | collective-permute-start | bytes 393224 | tf_op jit(solution)/shard_map/ppermute | solution.py:27
  35.1 7.2 %collective-permute-start.4 = (bf16[128,512]{1,0:T(8,128)(2,1)S(1)}, bf16[128,512]{1,0:T(8,128)(2,1)S(1)}, u32[]{:S(2)}, u32[]{:S(2)}) collective-permute-start(bf16[128,512]{1,0:T(8,128)(2,1)S(1)} %collective-permute-done.2), channel_id=1, source_target_pairs={{0,1},{1,2},{2,3},{3,4},{4,5},{5,6},{6,7},{7,8},{8,9},{9,10},{10,1... | collective-permute-start | bytes 393224 | tf_op jit(solution)/shard_map/ppermute | solution.py:21
  35.1 7.2 %collective-permute-start.5 = (bf16[128,512]{1,0:T(8,128)(2,1)S(1)}, bf16[128,512]{1,0:T(8,128)(2,1)S(1)}, u32[]{:S(2)}, u32[]{:S(2)}) collective-permute-start(bf16[128,512]{1,0:T(8,128)(2,1)S(1)} %collective-permute-done.3), channel_id=1, source_target_pairs={{0,15},{1,0},{2,1},{3,2},{4,3},{5,4},{6,5},{7,6},{8,7},{9,8},{10,9... | collective-permute-start | bytes 393224 | tf_op jit(solution)/shard_map/ppermute | solution.py:27
  42.3 7.2 %collective-permute-start.6 = (bf16[128,512]{1,0:T(8,128)(2,1)S(1)}, bf16[128,512]{1,0:T(8,128)(2,1)S(1)}, u32[]{:S(2)}, u32[]{:S(2)}) collective-permute-start(bf16[128,512]{1,0:T(8,128)(2,1)S(1)} %collective-permute-done.4), channel_id=1, source_target_pairs={{0,1},{1,2},{2,3},{3,4},{4,5},{5,6},{6,7},{7,8},{8,9},{9,10},{10,1... | collective-permute-start | bytes 393224 | tf_op jit(solution)/shard_map/ppermute | solution.py:21
  42.3 7.2 %collective-permute-start.7 = (bf16[128,512]{1,0:T(8,128)(2,1)S(1)}, bf16[128,512]{1,0:T(8,128)(2,1)S(1)}, u32[]{:S(2)}, u32[]{:S(2)}) collective-permute-start(bf16[128,512]{1,0:T(8,128)(2,1)S(1)} %collective-permute-done.5), channel_id=1, source_target_pairs={{0,15},{1,0},{2,1},{3,2},{4,3},{5,4},{6,5},{7,6},{8,7},{9,8},{10,9... | collective-permute-start | bytes 393224 | tf_op jit(solution)/shard_map/ppermute | solution.py:27
  49.5 7.2 %collective-permute-start.8 = (bf16[128,512]{1,0:T(8,128)(2,1)S(1)}, bf16[128,512]{1,0:T(8,128)(2,1)S(1)}, u32[]{:S(2)}, u32[]{:S(2)}) collective-permute-start(bf16[128,512]{1,0:T(8,128)(2,1)S(1)} %collective-permute-done.6), channel_id=1, source_target_pairs={{0,1},{1,2},{2,3},{3,4},{4,5},{5,6},{6,7},{7,8},{8,9},{9,10},{10,1... | collective-permute-start | bytes 393224 | tf_op jit(solution)/shard_map/ppermute | solution.py:21
  49.5 7.2 %collective-permute-start.9 = (bf16[128,512]{1,0:T(8,128)(2,1)S(1)}, bf16[128,512]{1,0:T(8,128)(2,1)S(1)}, u32[]{:S(2)}, u32[]{:S(2)}) collective-permute-start(bf16[128,512]{1,0:T(8,128)(2,1)S(1)} %collective-permute-done.7), channel_id=1, source_target_pairs={{0,15},{1,0},{2,1},{3,2},{4,3},{5,4},{6,5},{7,6},{8,7},{9,8},{10,9... | collective-permute-start | bytes 393224 | tf_op jit(solution)/shard_map/ppermute | solution.py:27
  56.7 7.2 %collective-permute-start.10 = (bf16[128,512]{1,0:T(8,128)(2,1)S(1)}, bf16[128,512]{1,0:T(8,128)(2,1)S(1)}, u32[]{:S(2)}, u32[]{:S(2)}) collective-permute-start(bf16[128,512]{1,0:T(8,128)(2,1)S(1)} %collective-permute-done.8), channel_id=1, source_target_pairs={{0,1},{1,2},{2,3},{3,4},{4,5},{5,6},{6,7},{7,8},{8,9},{9,10},{10,1... | collective-permute-start | bytes 393224 | tf_op jit(solution)/shard_map/ppermute | solution.py:21
  56.7 7.2 %collective-permute-start.11 = (bf16[128,512]{1,0:T(8,128)(2,1)S(1)}, bf16[128,512]{1,0:T(8,128)(2,1)S(1)}, u32[]{:S(2)}, u32[]{:S(2)}) collective-permute-start(bf16[128,512]{1,0:T(8,128)(2,1)S(1)} %collective-permute-done.9), channel_id=1, source_target_pairs={{0,15},{1,0},{2,1},{3,2},{4,3},{5,4},{6,5},{7,6},{8,7},{9,8},{10,9... | collective-permute-start | bytes 393224 | tf_op jit(solution)/shard_map/ppermute | solution.py:27
  63.9 7.1 %collective-permute-start.12 = (bf16[128,512]{1,0:T(8,128)(2,1)S(1)}, bf16[128,512]{1,0:T(8,128)(2,1)S(1)}, u32[]{:S(2)}, u32[]{:S(2)}) collective-permute-start(bf16[128,512]{1,0:T(8,128)(2,1)S(1)} %collective-permute-done.10), channel_id=1, source_target_pairs={{0,1},{1,2},{2,3},{3,4},{4,5},{5,6},{6,7},{7,8},{8,9},{9,10},{10,1... | collective-permute-start | bytes 393224 | tf_op jit(solution)/shard_map/ppermute | solution.py:21
  63.9 7.1 %collective-permute-start.13 = (bf16[128,512]{1,0:T(8,128)(2,1)S(1)}, bf16[128,512]{1,0:T(8,128)(2,1)S(1)}, u32[]{:S(2)}, u32[]{:S(2)}) collective-permute-start(bf16[128,512]{1,0:T(8,128)(2,1)S(1)} %collective-permute-done.11), channel_id=1, source_target_pairs={{0,15},{1,0},{2,1},{3,2},{4,3},{5,4},{6,5},{7,6},{8,7},{9,8},{10,9... | collective-permute-start | bytes 393224 | tf_op jit(solution)/shard_map/ppermute | solution.py:27
  71.0 7.1 %collective-permute-start.14 = (bf16[128,512]{1,0:T(8,128)(2,1)S(1)}, bf16[128,512]{1,0:T(8,128)(2,1)S(1)}, u32[]{:S(2)}, u32[]{:S(2)}) collective-permute-start(bf16[128,512]{1,0:T(8,128)(2,1)S(1)} %collective-permute-done.12), channel_id=1, source_target_pairs={{0,1},{1,2},{2,3},{3,4},{4,5},{5,6},{6,7},{7,8},{8,9},{9,10},{10,1... | collective-permute-start | bytes 393224 | tf_op jit(solution)/shard_map/ppermute | solution.py:21
  78.1 10.0 %slice-start = ((s8[16777216]{0:T(1024)(128)(4,1)}), s8[4194304]{0:T(1024)(128)(4,1)S(1)}, s32[]{:S(2)}) async-start(s8[16777216]{0:T(1024)(128)(4,1)} %bitcast.42), calls=%async_computation.4 | async-start | bytes 8388608
  79.6 8.5 %slice-start.1 = ((s8[16777216]{0:T(1024)(128)(4,1)}), s8[4194304]{0:T(1024)(128)(4,1)S(1)}, s32[]{:S(2)}) async-start(s8[16777216]{0:T(1024)(128)(4,1)} %bitcast.42), calls=%async_computation.5 | async-start | bytes 8388608
  79.6 8.5 %slice-start.2 = ((s8[16777216]{0:T(1024)(128)(4,1)}), s8[4194304]{0:T(1024)(128)(4,1)S(1)}, s32[]{:S(2)}) async-start(s8[16777216]{0:T(1024)(128)(4,1)} %bitcast.42), calls=%async_computation.6 | async-start | bytes 8388608
  79.6 9.5 %slice-start.3 = ((s8[16777216]{0:T(1024)(128)(4,1)}), s8[4194304]{0:T(1024)(128)(4,1)S(1)}, s32[]{:S(2)}) async-start(s8[16777216]{0:T(1024)(128)(4,1)} %bitcast.42), calls=%async_computation.7 | async-start | bytes 8388608
  79.6 9.5 %copy-start.5 = (bf16[128,1024]{1,0:T(8,128)(2,1)S(1)}, bf16[128,1024]{1,0:T(8,128)(2,1)}, u32[]{:S(2)}) copy-start(bf16[128,1024]{1,0:T(8,128)(2,1)} %param.8) | copy-start | bytes 786436
  96.7 147.3 %reduce-scatter.3.cloned.1.call-start = ((), (), s32[]{:S(2)}) async-start(), calls=%async_computation.2 | async-start | bytes 4456448 | tf_op jit(solution)/shard_map/reduce_scatter | solution.py:116
Sparse Core Ops, SparseCore 0:
  96.8 71.1 reduce-scatter.4
  172.3 71.6 reduce-scatter.2
